TPU v7x, 512 devices: a whole 4x8x8 slice. The times are simulated.
512 devices in a mesh: chan: 32 (over z_hi, y, core), tm: 16 (over z_lo, x).
Axes of the slice: x: 4, y: 8, z: 8 (z_hi: 2, z_lo: 4; z = z_hi * 4 + z_lo), core: 2. Of those that a mesh axis runs over, the one named last changes fastest.
Arguments:
- recordings: bfloat16 [1024, 192, 4096], P('chan', 'tm'), may hold values from -6 to 6
- valid_mask: int32 [1024, 192], P('chan', 'tm'), may hold values 0 or 1
- src_chan: int32 [4], replicated, may hold values from 0 to 1023
Outputs:
- stacks: float32 [4, 1024, 4096], P(None, ('chan', 'tm'))
All inputs are finite; a program needn't handle non-finite values. No bound on the sum of `valid_mask` on one device may be relied on, other than what follows from the above.
Results may differ from a plain program's by a relative error of at most 0.0048.
Values may be sent and summed in bfloat16 or wider, within the bound.
A program may use at most 128 MiB of HBM per device.

v0:
```python
import math

import jax
import jax.numpy as jnp
from jax import lax
from jax.sharding import PartitionSpec as P

NSRC = 4
SLOW = 32
FAST = 128


def spread(block, axis, holder):
    block = jnp.where(lax.axis_index(axis) == holder, block, jnp.zeros_like(block))
    return lax.psum(block, axis)


def angles(rows_count, cols_count, period):
    left_index = jnp.arange(rows_count, dtype=jnp.int32)[:, None]
    right_index = jnp.arange(cols_count, dtype=jnp.int32)[None, :]
    return 2.0 * math.pi / period * (left_index * right_index % period).astype(jnp.float32)


def forward(tiles):
    slow_len = tiles.shape[1]
    fast_len = tiles.shape[2]
    samples = slow_len * fast_len
    slow_angle = angles(slow_len, slow_len, slow_len)
    cos_slow = jnp.cos(slow_angle).astype(jnp.bfloat16)
    sin_slow = jnp.sin(slow_angle).astype(jnp.bfloat16)
    real_part = jnp.einsum("kn,rnm->rkm", cos_slow, tiles, preferred_element_type=jnp.float32)
    imag_part = -jnp.einsum("kn,rnm->rkm", sin_slow, tiles, preferred_element_type=jnp.float32)
    twist = angles(slow_len, fast_len, samples)
    twist_cos = jnp.cos(twist)
    twist_sin = jnp.sin(twist)
    z_real = (real_part * twist_cos + imag_part * twist_sin).astype(jnp.bfloat16)
    z_imag = (imag_part * twist_cos - real_part * twist_sin).astype(jnp.bfloat16)
    fast_angle = angles(fast_len, fast_len, fast_len)
    cos_fast = jnp.cos(fast_angle).astype(jnp.bfloat16)
    sin_fast = jnp.sin(fast_angle).astype(jnp.bfloat16)
    x_real = jnp.einsum(
        "rkn,nm->rkm", z_real, cos_fast, preferred_element_type=jnp.float32
    ) + jnp.einsum("rkn,nm->rkm", z_imag, sin_fast, preferred_element_type=jnp.float32)
    x_imag = jnp.einsum(
        "rkn,nm->rkm", z_imag, cos_fast, preferred_element_type=jnp.float32
    ) - jnp.einsum("rkn,nm->rkm", z_real, sin_fast, preferred_element_type=jnp.float32)
    power = x_real * x_real + x_imag * x_imag
    band_mean = jnp.mean(power, axis=1)
    row_count = band_mean.shape[0]
    band_mean = jnp.mean(band_mean.reshape(row_count, fast_len // 2, 2), axis=2)
    band_mean = jnp.repeat(band_mean, 2, axis=1)
    whiten_scale = lax.rsqrt(band_mean + 1e-06)[:, None, :]
    return (
        (x_real * whiten_scale).astype(jnp.bfloat16),
        (x_imag * whiten_scale).astype(jnp.bfloat16),
    )


def inverse(z_real, z_imag, out_scale):
    slow_len = z_real.shape[-2]
    fast_len = z_real.shape[-1]
    samples = slow_len * fast_len
    back_angle = angles(fast_len, fast_len, fast_len)
    back_cos = jnp.cos(back_angle)
    back_sin = jnp.sin(back_angle)
    high = lax.Precision.HIGHEST
    v_real = jnp.einsum("...kn,nb->...kb", z_real, back_cos, precision=high) - jnp.einsum(
        "...kn,nb->...kb", z_imag, back_sin, precision=high
    )
    v_imag = jnp.einsum("...kn,nb->...kb", z_real, back_sin, precision=high) + jnp.einsum(
        "...kn,nb->...kb", z_imag, back_cos, precision=high
    )
    twist = angles(slow_len, fast_len, samples)
    twist_cos = jnp.cos(twist)
    twist_sin = jnp.sin(twist)
    w_real = v_real * twist_cos - v_imag * twist_sin
    w_imag = v_real * twist_sin + v_imag * twist_cos
    outer_angle = angles(slow_len, slow_len, slow_len)
    lagged = jnp.einsum(
        "ak,...kb->...ab", jnp.cos(outer_angle), w_real, precision=high
    ) - jnp.einsum("ak,...kb->...ab", jnp.sin(outer_angle), w_imag, precision=high)
    return lagged * out_scale


def per_device(recordings, valid_mask, src_chan):
    chan_count = recordings.shape[0]
    seg_count = recordings.shape[1]
    samples = recordings.shape[2]
    group_count = lax.axis_size("tm")
    tiled = recordings.reshape(chan_count, seg_count, SLOW, FAST)
    src_owner = src_chan // chan_count
    src_row = src_chan % chan_count
    out_scale = 1.0 / math.sqrt(samples * seg_count * group_count)
    src_tiles = []
    src_flags = []
    for source in range(NSRC):
        own_tiles = lax.dynamic_index_in_dim(tiled, src_row[source], 0, keepdims=False)
        own_flags = lax.dynamic_index_in_dim(valid_mask, src_row[source], 0, keepdims=False)
        got_tiles, got_flags = (
            spread(own_tiles, "chan", src_owner[source]),
            spread(own_flags, "chan", src_owner[source]),
        )
        src_tiles.append(got_tiles)
        src_flags.append(got_flags)
    joined = jnp.concatenate([tiled, jnp.stack(src_tiles, axis=0)], axis=0)

    def one_segment(segment):
        return forward(lax.dynamic_index_in_dim(joined, segment, 1, keepdims=False))

    white_real, white_imag = lax.map(one_segment, jnp.arange(seg_count, dtype=jnp.int32))
    rec_real = white_real[:, :chan_count]
    rec_imag = white_imag[:, :chan_count]
    src_real = white_real[:, chan_count:]
    src_imag = white_imag[:, chan_count:]
    src_valid = jnp.stack(src_flags, axis=1)
    src_weight = src_valid.astype(jnp.float32)[:, :, None, None]
    rec_weight = jnp.transpose(valid_mask).astype(jnp.float32)[:, :, None, None]
    src_real_w = (src_real.astype(jnp.float32) * src_weight)[:, :, None]
    src_imag_w = (src_imag.astype(jnp.float32) * src_weight)[:, :, None]
    rec_real_w = (rec_real.astype(jnp.float32) * rec_weight)[:, None]
    rec_imag_w = (rec_imag.astype(jnp.float32) * rec_weight)[:, None]
    cross_real = jnp.sum(src_real_w * rec_real_w + src_imag_w * rec_imag_w, axis=0)
    cross_imag = jnp.sum(src_real_w * rec_imag_w - src_imag_w * rec_real_w, axis=0)
    lagged = inverse(cross_real, cross_imag, out_scale)
    summed = jnp.sum(
        lax.all_to_all(lagged[None], "tm", split_axis=2, concat_axis=0, tiled=True), axis=0
    )
    return summed.reshape(NSRC, chan_count // group_count, samples)


def solution(mesh):
    return jax.shard_map(
        per_device,
        mesh=mesh,
        in_specs=(P("chan", "tm", None), P("chan", "tm"), P()),
        out_specs=P(None, ("chan", "tm"), None),
        check_vma=False,
    )
```

profile of v0, /device:TPU:57, one launch (start us, length us, event | category | flops | bytes accessed | tf_op | source)
XLA Modules:
  0.0 555.1 jit_solution(12261258882971634843)
XLA Ops:
  6.5 0.7 and_select_fusion.1
  7.2 0.7 fusion.143
  15.3 2.7 copy.25
  20.4 0.8 dynamic-slice_select_fusion
  21.5 17.5 %all-reduce = (s32[12,1]{0,1:T(1,128)S(1)}, s32[12,1]{0,1:T(1,128)S(1)}, s32[12,1]{0,1:T(1,128)S(1)}, s32[12,1]{0,1:T(1,128)S(1)}) all-reduce(s32[12,1]{0,1:T(1,128)S(1)} %bitcast.144, s32[12,1]{0,1:T(1,128)S(1)} %bitcast.142, s32[12,1]{0,1:T(1,128)S(1)} %bitcast.143, ...), channel_id=1, replica_groups=mesh['chan'=32,'tm'=16] {'chan'}, use_global_device_ids=true, to_apply=%region_11.12 | all-reduce | flops 48 | bytes 384 | tf_op jit(solution)/shard_map/psum | solution.py:15
  39.2 2.4 constant_dynamic-update-slice_fusion.4
  41.6 317.3 %all-reduce.4.cloned.1.call-done = (bf16[1,12,32,128]{3,2,0,1:T(8,128)(2,1)}, bf16[1,12,32,128]{3,2,0,1:T(8,128)(2,1)}, bf16[1,12,32,128]{3,2,0,1:T(8,128)(2,1)}, bf16[1,12,32,128]{3,2,0,1:T(8,128)(2,1)}) async-done(((bf16[1,12,32,128]{3,2,0,1:T(8,128)(2,1)}, bf16[1,12,32,128]{3,2,0,1:T(8,128)(2,1)}, bf16[1,12,32,128]{3,2,0,1:T(8,128)(2,1)}, bf16[1,12,32,128]{3,2,0,1:T(8,128)(2,1)}), ...) | async-done | bytes 393232 | tf_op jit(solution)/shard_map/psum | solution.py:15
  359.0 1.6 constant_dynamic-update-slice_fusion.3
  360.5 1.6 constant_dynamic-update-slice_fusion.2
  362.1 1.6 constant_dynamic-update-slice_fusion.1
  363.6 1.6 constant_dynamic-update-slice_fusion
  365.2 101.3 %while.15 = (s32[]{:T(128)}, bf16[12,36,32,128]{3,2,1,0:T(8,128)(2,1)}, bf16[12,36,32,128]{3,2,1,0:T(8,128)(2,1)}, s32[12]{0:T(128)S(1)}, bf16[36,12,32,128]{3,2...) while((s32[]{:T(128)}, bf16[12,36,32,128]{3,2,1,0:T(8,128)(2,1)}, ...), condition=%wide.region_7.8_spmd, body=%wide.region_4.7_spmd.sunk | while | flops 173748992 | bytes 9724567 | solution.py:110
  365.2 0.6 dynamic_slice.73
  367.7 1.3 fusion.176
  369.1 1.3 subtract_convert_fusion.2
  372.7 1.0 fusion.180
  376.2 1.2 fusion.176
  377.5 1.3 subtract_convert_fusion.2
  381.1 1.0 fusion.180
  384.6 1.2 fusion.176
  386.0 1.3 subtract_convert_fusion.2
  389.5 1.0 fusion.180
  390.5 0.6 dynamic_slice.73
  393.0 1.3 fusion.176
  394.4 1.3 subtract_convert_fusion.2
  398.0 1.0 fusion.180
  398.9 0.6 dynamic_slice.73
  401.5 1.3 fusion.176
  402.8 1.3 subtract_convert_fusion.2
  406.4 1.0 fusion.180
  409.9 1.2 fusion.176
  411.2 1.3 subtract_convert_fusion.2
  414.8 1.0 fusion.180
  415.8 0.6 dynamic_slice.73
  418.3 1.2 fusion.176
  419.7 1.3 subtract_convert_fusion.2
  423.3 1.0 fusion.180
  424.3 0.6 dynamic_slice.73
  426.8 1.2 fusion.176
  428.1 1.3 subtract_convert_fusion.2
  431.7 1.0 fusion.180
  435.2 1.3 fusion.176
  436.6 1.3 subtract_convert_fusion.2
  440.2 1.0 fusion.180
  443.7 1.2 fusion.176
  445.0 1.3 subtract_convert_fusion.2
  448.6 1.0 fusion.180
  452.1 1.3 fusion.176
  453.5 1.3 subtract_convert_fusion.2
  457.0 1.0 fusion.180
  460.6 1.2 fusion.176
  461.9 1.3 subtract_convert_fusion.2
  465.5 1.0 fusion.180
  466.5 1.3 convert_multiply_fusion.3
  467.8 3.4 convert_multiply_fusion.1
  471.1 8.7 %subtract_reduce_fusion = (f32[4,32,32,128]{3,2,1,0:T(8,128)S(1)}, f32[4,32,32,128]{3,2,1,0:T(8,128)S(1)}) fusion(f32[12,32,32,128]{3,2,1,0:T(8,128)S(1)} %get-tuple-element.138, f32[12,4,32,128]{3,2,1,0:T(8,128)S(1)} %get-tuple-element.136, f32[12,32,32,128]{3,2,1,0:T(8,128)S(1)} %get-tuple-element.137, f32[12,4,32,128]{3,2,1,0:T(8,128)S(1)} %get-tuple-element.135), kind=kLoop, calls=%fused_computation.83 | loop fusion | flops 49283072 | bytes 18350080 | tf_op jit(solution)/shard_map/reduce_sum | solution.py:123
  479.9 2.1 fusion.85
  482.0 2.1 fusion.87
  484.1 2.1 convolution_subtract_fusion.1
  486.2 2.1 convolution_add_fusion.1
  488.3 2.2 fusion.67
  490.5 2.3 multiply_bitcast_fusion
  493.1 54.2 %all_to_all.12 = f32[1,4,32,32,128]{4,3,1,0,2:T(8,128)S(1)} all-to-all(f32[1,4,32,32,128]{4,3,1,0,2:T(8,128)S(1)} %copy.19), channel_id=1, replica_groups=mesh['chan'=32,'tm'=16] {'tm'}, dimensions={2} | all-to-all | bytes 4194304 | tf_op jit(solution)/shard_map/all_to_all | solution.py:126
  547.5 0.8 copy.20
  (154 shorter events, 32.3 us)
Async XLA Ops:
  6.5 352.4 %all-reduce.4.cloned.1.call-start = ((), (), s32[]{:S(2)}) async-start(), calls=%async_computation.1 | async-start | bytes 786432 | tf_op jit(solution)/shard_map/psum | solution.py:15
  15.3 6.1 %copy-start = (s32[32,12]{0,1:T(8,128)S(1)}, s32[32,12]{0,1:T(8,128)}, u32[]{:S(2)}) copy-start(s32[32,12]{0,1:T(8,128)} %param.6) | copy-start | bytes 4612
Sparse Core Ops, SparseCore 0:
  21.3 337.6 all-reduce.3
where the time goes:
time: 557 us; the launch traced here: 555 us
  waiting for transfers between devices  317 us (57%)
  blocking collectives  71.8 us (13%)
  matrix products  66.6 us (12%)
  other arithmetic  29.3 us (5%)
  loops' own time  24.2 us (4%)
  between operations  23.3 us (4%)
  local copies, waits for them, and re-layouts  22.5 us (4%)
    psum x1, waiting for transfers between devices, spread(): return lax.psum(block, axis)  317 us
    all_to_all x1, blocking collectives, per_device(): lax.all_to_all(lagged[None], 'tm', split_axis=2, concat_axis=0, tiled=True)  54.2 us
    another operation x1, loops' own time, per_device(): lax.map(one_segment, jnp.arange(seg_count, dtype=jnp.int32))  24.2 us
    psum x1, blocking collectives, spread(): return lax.psum(block, axis)  17.5 us
    dot_general x12, matrix products, forward(): jnp.einsum('kn,rnm->rkm', cos_slow, tiles, preferred_element_type=jnp.flo...  15.9 us
    dot_general x12, matrix products, forward(): jnp.einsum('kn,rnm->rkm', sin_slow, tiles, preferred_element_type=jnp.flo...  15 us
    dynamic_update_slice x12, other arithmetic, per_device(): lax.map(one_segment, jnp.arange(seg_count, dtype=jnp.int32))  11.8 us
  transfers between devices with their start and end apart: 1, of which 1 were waited for; matrix products, arithmetic and copies ran while one was open for 1% of the time, Pallas kernels for 0%

commit v1 on v0

v1 whole, which is shorter than its diff:
```python
import functools
import math

import jax
import jax.numpy as jnp
import numpy as np
from jax import lax
from jax.experimental import pallas as pl
from jax.experimental.pallas import tpu as pltpu
from jax.sharding import PartitionSpec as P

NSRC = 4
SLOW = 32
FAST = 128
BLOCK = 4
MESH = pl.DeviceIdType.MESH
VMEM_LIMIT = 60 * 1024 * 1024


def angles(rows_count, cols_count, period):
    left_index = np.arange(rows_count)[:, None]
    right_index = np.arange(cols_count)[None, :]
    return 2.0 * math.pi / period * (left_index * right_index % period)


def tables(out_scale):
    slow = angles(SLOW, SLOW, SLOW)
    fast = angles(FAST, FAST, FAST)
    twist = angles(SLOW, FAST, SLOW * FAST)
    first = np.kron(np.eye(8), np.concatenate([np.cos(slow), -np.sin(slow)], axis=0))
    second = np.block([[np.cos(fast), -np.sin(fast)], [np.sin(fast), np.cos(fast)]])
    back = np.block([[np.cos(fast), np.sin(fast)], [-np.sin(fast), np.cos(fast)]])
    outer = np.concatenate(
        [np.kron(np.eye(NSRC), np.cos(slow)), np.kron(np.eye(NSRC), -np.sin(slow))], axis=1
    )
    return (
        jnp.asarray(first, jnp.bfloat16),
        jnp.asarray(second, jnp.bfloat16),
        jnp.asarray(back, jnp.bfloat16),
        jnp.asarray(outer, jnp.bfloat16),
        jnp.asarray(np.stack([np.cos(twist), np.sin(twist)]), jnp.float32),
        jnp.asarray(np.stack([np.cos(twist), np.sin(twist)]) * out_scale, jnp.float32),
    )


def exchange(source, target, send, recv, device):
    return pltpu.make_async_remote_copy(
        src_ref=source,
        dst_ref=target,
        send_sem=send,
        recv_sem=recv,
        device_id=device,
        device_id_type=MESH,
    )


def greet(devices):
    barrier = pltpu.get_barrier_semaphore()
    for device in devices:
        pl.semaphore_signal(barrier, inc=1, device_id=device, device_id_type=MESH)
    pl.semaphore_wait(barrier, len(devices))


def share_kernel(
    ycount, own, out, pair_in, half, slices_in, part, across_in, whole, twin, s1, r1, s2, r2, s3, r3, s4, r4, s5, r5
):
    me = lax.axis_index("chan")
    core = me % 2
    y = me // 2 % ycount
    z = me // (2 * ycount)
    sibling = {"chan": me - core + (1 - core)}
    opposite = {"chan": ((1 - z) * ycount + y) * 2 + core}

    def along(step):
        return (y + step) % ycount

    def at(place):
        return {"chan": (z * ycount + place) * 2 + core}

    greet([sibling, opposite] + [at(along(step)) for step in range(1, ycount)])

    copy = exchange(own.at[1 - core], pair_in, s1, r1, sibling)
    copy.start()
    copy.wait()
    half[...] = own[core] + pair_in[...]

    copies = []
    for step in range(1, ycount):
        copies.append(
            exchange(
                half.at[along(step)],
                slices_in.at[step - 1],
                s2.at[step - 1],
                r2.at[step - 1],
                at(along(step)),
            )
        )
        copies[-1].start()
    for copy in copies:
        copy.wait()
    total = half[y]
    for step in range(ycount - 1):
        total = total + slices_in[step]
    part[...] = total

    copy = exchange(part, across_in, s3, r3, opposite)
    copy.start()
    copy.wait()
    whole[y] = part[...] + across_in[...]

    copies = []
    for step in range(1, ycount):
        copies.append(
            exchange(whole.at[y], whole.at[y], s4.at[step - 1], r4.at[step - 1], at(along(step)))
        )
        copies[-1].start()
    for copy in copies:
        copy.wait()

    copy = exchange(whole, twin, s5, r5, sibling)
    copy.start()
    out[core] = whole[...]
    copy.wait()
    out[1 - core] = twin[...]


def share(own, ycount):
    rows = own.shape[0]
    per = rows // (2 * ycount)
    shaped = own.reshape(2, ycount, per, FAST)
    half = (ycount, per, FAST)
    dma = pltpu.SemaphoreType.DMA
    spec = pl.BlockSpec(memory_space=pltpu.VMEM)
    out = pl.pallas_call(
        functools.partial(share_kernel, ycount),
        out_shape=jax.ShapeDtypeStruct(shaped.shape, own.dtype),
        in_specs=[spec],
        out_specs=spec,
        scratch_shapes=[
            pltpu.VMEM(half, own.dtype),
            pltpu.VMEM(half, own.dtype),
            pltpu.VMEM((ycount - 1, per, FAST), own.dtype),
            pltpu.VMEM((per, FAST), own.dtype),
            pltpu.VMEM((per, FAST), own.dtype),
            pltpu.VMEM(half, own.dtype),
            pltpu.VMEM(half, own.dtype),
            dma,
            dma,
            dma((ycount - 1,)),
            dma((ycount - 1,)),
            dma,
            dma,
            dma((ycount - 1,)),
            dma((ycount - 1,)),
            dma,
            dma,
        ],
        compiler_params=pltpu.CompilerParams(
            collective_id=0, has_side_effects=True, vmem_limit_bytes=VMEM_LIMIT
        ),
        name="share",
    )(shaped)
    return out.reshape(rows, FAST)


def gather_kernel(xcount, zcount, parts, out, x_in, mid, z_in, s1, r1, s2, r2):
    me = lax.axis_index("tm")
    x = me % xcount
    z = me // xcount

    def at(zpos, xpos):
        return {"tm": zpos * xcount + xpos}

    greet(
        [at(z, (x + step) % xcount) for step in range(1, xcount)]
        + [at((z + step) % zcount, x) for step in range(1, zcount)]
    )
    copies = []
    for step in range(1, xcount):
        to = (x + step) % xcount
        copies.append(
            exchange(parts.at[to], x_in.at[step - 1], s1.at[step - 1], r1.at[step - 1], at(z, to))
        )
        copies[-1].start()
    for copy in copies:
        copy.wait()

    def add_up(place):
        total = parts[x, place].astype(jnp.float32)
        for step in range(xcount - 1):
            total = total + x_in[step, place].astype(jnp.float32)
        return total

    copies = []
    for step in range(1, zcount):
        to = (z + step) % zcount
        mid[step - 1] = add_up(to).astype(jnp.bfloat16)
        copies.append(
            exchange(mid.at[step - 1], z_in.at[step - 1], s2.at[step - 1], r2.at[step - 1], at(to, x))
        )
        copies[-1].start()
    total = add_up(z)
    for copy in copies:
        copy.wait()
    for step in range(zcount - 1):
        total = total + z_in[step].astype(jnp.float32)
    out[...] = total


def gather(parts):
    xcount, zcount = parts.shape[:2]
    block = parts.shape[2:]
    dma = pltpu.SemaphoreType.DMA
    spec = pl.BlockSpec(memory_space=pltpu.VMEM)
    return pl.pallas_call(
        functools.partial(gather_kernel, xcount, zcount),
        out_shape=jax.ShapeDtypeStruct(block, jnp.float32),
        in_specs=[spec],
        out_specs=spec,
        scratch_shapes=[
            pltpu.VMEM((xcount - 1, zcount) + block, parts.dtype),
            pltpu.VMEM((zcount - 1,) + block, parts.dtype),
            pltpu.VMEM((zcount - 1,) + block, parts.dtype),
            dma((xcount - 1,)),
            dma((xcount - 1,)),
            dma((zcount - 1,)),
            dma((zcount - 1,)),
        ],
        compiler_params=pltpu.CompilerParams(
            collective_id=1, has_side_effects=True, vmem_limit_bytes=VMEM_LIMIT
        ),
        name="gather",
    )(parts)


def transform(tiles, weight, first, second, twist, keep):
    segs = tiles.shape[0] // SLOW
    lane = lax.broadcasted_iota(jnp.int32, (8, FAST), 1)
    for pair in range(segs // 16):
        base = pair * 512
        wide = jnp.concatenate(
            [tiles[pl.ds(base, 256), :], tiles[pl.ds(base + 256, 256), :]], axis=1
        )
        mixed = jnp.dot(first[...], wide, preferred_element_type=jnp.float32)
        for side in range(2):
            group = mixed[:, side * FAST : (side + 1) * FAST].reshape(8, 2 * SLOW, FAST)
            real_part = group[:, :SLOW]
            imag_part = group[:, SLOW:]
            twist_cos = twist[0][None]
            twist_sin = twist[1][None]
            z_real = (real_part * twist_cos + imag_part * twist_sin).astype(jnp.bfloat16)
            z_imag = (imag_part * twist_cos - real_part * twist_sin).astype(jnp.bfloat16)
            joined = jnp.concatenate([z_real, z_imag], axis=2).reshape(8 * SLOW, 2 * FAST)
            bins = jnp.dot(joined, second[...], preferred_element_type=jnp.float32)
            x_real = bins[:, :FAST].reshape(8, SLOW, FAST)
            x_imag = bins[:, FAST:].reshape(8, SLOW, FAST)
            power = jnp.sum(x_real * x_real + x_imag * x_imag, axis=1)
            other = jnp.where(
                lane % 2 == 0, pltpu.roll(power, FAST - 1, 1), pltpu.roll(power, 1, 1)
            )
            scale = lax.rsqrt((power + other) * (1.0 / (2 * SLOW)) + 1e-06)
            at = pair * 16 + side * 8
            if weight is not None:
                scale = scale * weight[pl.ds(at, 8), :]
            scale = scale[:, None, :]
            keep[0, pl.ds(at, 8)] = (x_real * scale).astype(jnp.bfloat16).astype(jnp.float32)
            keep[1, pl.ds(at, 8)] = (x_imag * scale).astype(jnp.bfloat16).astype(jnp.float32)


def stack_kernel(
    seg_count, tiles, weight, shared, first, second, back, outer, twist, turn, out, white, source
):
    @pl.when(pl.program_id(0) == 0)
    def _():
        transform(shared, None, first, second, twist, source)

    transform(tiles, weight, first, second, twist, white)

    def one_channel(chan, carry):
        strips = []
        for strip in range(SLOW // 8):
            rows = pl.ds(strip * 8, 8)
            real_sum = [None] * NSRC
            imag_sum = [None] * NSRC
            for seg in range(seg_count):
                w_real = white[0, chan * seg_count + seg, rows]
                w_imag = white[1, chan * seg_count + seg, rows]
                for src in range(NSRC):
                    s_real = source[0, src * seg_count + seg, rows]
                    s_imag = source[1, src * seg_count + seg, rows]
                    real_now = s_real * w_real + s_imag * w_imag
                    imag_now = s_real * w_imag - s_imag * w_real
                    first_seg = real_sum[src] is None
                    real_sum[src] = real_now if first_seg else real_sum[src] + real_now
                    imag_sum[src] = imag_now if first_seg else imag_sum[src] + imag_now
            strips.append((real_sum, imag_sum))
        cross_real = jnp.concatenate(
            [strips[k][0][src] for src in range(NSRC) for k in range(SLOW // 8)], axis=0
        )
        cross_imag = jnp.concatenate(
            [strips[k][1][src] for src in range(NSRC) for k in range(SLOW // 8)], axis=0
        )
        both = jnp.concatenate(
            [cross_real.astype(jnp.bfloat16), cross_imag.astype(jnp.bfloat16)], axis=1
        )
        v = jnp.dot(both, back[...], preferred_element_type=jnp.float32)
        v_real = v[:, :FAST].reshape(NSRC, SLOW, FAST)
        v_imag = v[:, FAST:].reshape(NSRC, SLOW, FAST)
        turn_cos = turn[0][None]
        turn_sin = turn[1][None]
        w_real = (v_real * turn_cos - v_imag * turn_sin).astype(jnp.bfloat16)
        w_imag = (v_real * turn_sin + v_imag * turn_cos).astype(jnp.bfloat16)
        tall = jnp.concatenate(
            [w_real.reshape(NSRC * SLOW, FAST), w_imag.reshape(NSRC * SLOW, FAST)], axis=0
        )
        lagged = jnp.dot(outer[...], tall, preferred_element_type=jnp.float32)
        out[chan // 2, 0, chan % 2] = lagged.astype(jnp.bfloat16).reshape(NSRC, SLOW, FAST)
        return carry

    lax.fori_loop(0, BLOCK, one_channel, 0)


def stack(tiles, weight, shared, chan_count, seg_count, xcount, zcount, out_scale):
    per = chan_count // (xcount * zcount)
    block_rows = BLOCK * seg_count * SLOW
    consts = tables(out_scale)
    turns = xcount // 2

    def whole(array):
        zeros = (0,) * array.ndim
        return pl.BlockSpec(array.shape, lambda i: zeros)

    return pl.pallas_call(
        functools.partial(stack_kernel, seg_count),
        grid=(chan_count // BLOCK,),
        out_shape=jax.ShapeDtypeStruct((xcount, zcount, per, NSRC, SLOW, FAST), jnp.bfloat16),
        in_specs=[
            pl.BlockSpec((block_rows, FAST), lambda i: (i, 0)),
            pl.BlockSpec((BLOCK * seg_count, FAST), lambda i: (i, 0)),
            whole(shared),
        ]
        + [whole(const) for const in consts],
        out_specs=pl.BlockSpec(
            (2, 1, per, NSRC, SLOW, FAST), lambda i: (i % turns, i // turns, 0, 0, 0, 0)
        ),
        scratch_shapes=[
            pltpu.VMEM((2, BLOCK * seg_count, SLOW, FAST), jnp.float32),
            pltpu.VMEM((2, NSRC * seg_count, SLOW, FAST), jnp.float32),
        ],
        compiler_params=pltpu.CompilerParams(
            dimension_semantics=("arbitrary",), vmem_limit_bytes=VMEM_LIMIT
        ),
        name="stack",
    )(tiles, weight, shared, *consts)


def per_device(recordings, valid_mask, src_chan):
    chan_count, seg_count, samples = recordings.shape
    group_count = lax.axis_size("tm")
    xcount = 4
    zcount = group_count // xcount
    ycount = lax.axis_size("chan") // 4
    tiled = recordings.reshape(chan_count, seg_count, SLOW, FAST)
    src_owner = src_chan // chan_count
    src_row = src_chan % chan_count
    out_scale = 1.0 / math.sqrt(samples * seg_count * group_count)
    mine = []
    for source in range(NSRC):
        own = lax.dynamic_index_in_dim(tiled, src_row[source], 0, keepdims=False)
        flags = lax.dynamic_index_in_dim(valid_mask, src_row[source], 0, keepdims=False)
        here = (flags != 0) & (lax.axis_index("chan") == src_owner[source])
        mine.append(jnp.where(here[:, None, None], own, jnp.zeros_like(own)))
    shared = share(jnp.stack(mine).reshape(NSRC * seg_count * SLOW, FAST), ycount)
    weight = jnp.broadcast_to(
        valid_mask.astype(jnp.float32).reshape(chan_count * seg_count, 1),
        (chan_count * seg_count, FAST),
    )
    parts = stack(
        tiled.reshape(chan_count * seg_count * SLOW, FAST),
        weight,
        shared,
        chan_count,
        seg_count,
        xcount,
        zcount,
        out_scale,
    )
    summed = gather(parts)
    return jnp.transpose(summed, (1, 0, 2, 3)).reshape(NSRC, chan_count // group_count, samples)


def solution(mesh):
    return jax.shard_map(
        per_device,
        mesh=mesh,
        in_specs=(P("chan", "tm", None), P("chan", "tm"), P()),
        out_specs=P(None, ("chan", "tm"), None),
        check_vma=False,
    )
```

time: 557 us -> 126 us (0.23)
  the two profiles are of different devices: /device:TPU:57 before, /device:TPU:1 now
where the time goes in v1:
time: 126 us; the launch traced here: 125 us
  Pallas kernels  94 us (75%)
  local copies, waits for them, and re-layouts  18.5 us (15%)
  between operations  10.2 us (8%)
  other arithmetic  2.21 us (2%)
    pallas_call x1, Pallas kernels, share(): pl.pallas_call(functools.partial(share_kernel, ycount), out_shape=jax.Sha...  37.1 us
    pallas_call x1, Pallas kernels, stack(): pl.pallas_call(functools.partial(stack_kernel, seg_count), grid=(chan_cou...  31.3 us
    pallas_call x1, Pallas kernels, gather(): pl.pallas_call(functools.partial(gather_kernel, xcount, zcount), out_shap...  25.6 us
    unnamed x8, local copies, waits for them, and re-layouts  8.15 us
    another operation x1, local copies, waits for them, and re-layouts, per_device(): tiled.reshape(chan_count * seg_count * SLOW, FAST)  6.96 us

profile of v1, /device:TPU:1, one launch (start us, length us, event | category | flops | bytes accessed | tf_op | source)
XLA Modules:
  0.0 125.0 jit_solution(15354198602156083717)
XLA Ops:
  0.0 5.6 %copy.16 = bf16[32,12,4096]{2,1,0:T(8,128)(2,1)} copy(bf16[32,12,4096]{2,0,1:T(8,128)(2,1)} %param.9) | data formatting | bytes 6291456 | tf_op args[0]
  5.6 0.0 copy-start.1
  5.6 0.0 copy-start
  5.6 7.0 %reshape_reshape.6.tiles = bf16[12288,128]{1,0:T(8,128)(2,1)} reshape(bf16[32,12,4096]{2,1,0:T(8,128)(2,1)} %copy.16) | data formatting | bytes 6291456 | tf_op jit(solution)/shard_map/reshape;reshape | solution.py:379
  12.6 0.0 copy-done.1
  12.6 0.1 copy.17
  12.7 0.1 broadcast_in_dim.34
  12.8 0.8 broadcast_in_dim.35.weight
  13.6 0.0 copy-done
  13.6 0.0 copy-start.2
  13.6 2.5 %copy.27 = bf16[48,8,32,128]{3,2,1,0:T(8,128)(2,1)} copy(bf16[48,8,32,128]{3,1,2,0:T(8,128)(2,1)S(1)} %bitcast.29) | data formatting | bytes 6291456
  16.1 0.0 copy-done.2
  16.1 0.7 fusion.8
  27.0 0.2 fusion.7
  27.2 1.2 bitcast_select_fusion.3
  28.4 0.8 pad_maximum_fusion
  29.2 37.1 %share.1 = bf16[2,8,96,128]{3,2,1,0:T(8,128)(2,1)} custom-call(bf16[2,8,96,128]{3,2,1,0:T(8,128)(2,1)} %bitcast.31), custom_call_target="tpu_custom_call" | custom-call | tf_op jit(solution)/shard_map/share/pallas_call | solution.py:134
  66.3 31.3 %stack.4.parts = bf16[4,4,2,4,32,128]{5,4,3,2,1,0:T(8,128)(2,1)} custom-call(bf16[12288,128]{1,0:T(8,128)(2,1)} %reshape_reshape.6.tiles, f32[384,128]{1,0:T(8,128)} %broadcast_in_dim.35.weight, bf16[1536,128]{1,0:T(8,128)(2,1)} %bitcast.32, bf16[512,256]{1,0:T(8,128)(2,1)} %constant.69.clone.first, bf16[256,256]{1,0:T(8,128)(2,1)} %constant.70.clone.second, ...), custom_call_target="tpu_custom_call" | custom-call | tf_op jit(solution)/shard_map/stack/pallas_call | solution.py:333
  97.6 25.6 %gather.1 = f32[2,4,32,128]{3,2,1,0:T(8,128)} custom-call(bf16[4,4,2,4,32,128]{5,4,3,2,1,0:T(8,128)(2,1)} %stack.4.parts), custom_call_target="tpu_custom_call" | custom-call | tf_op jit(solution)/shard_map/gather/pallas_call | solution.py:215
  123.2 0.9 reshape.53
  124.2 0.8 copy.22
  (2 shorter events, 0.0 us)
Async XLA Ops:
  5.6 7.0 %copy-start.1 = (s32[32,12]{0,1:T(8,128)S(1)}, s32[32,12]{0,1:T(8,128)}, u32[]{:S(2)}) copy-start(s32[32,12]{0,1:T(8,128)} %param.10) | copy-start | bytes 4612
  5.6 8.0 %copy-start = (bf16[32,12,4096]{2,0,1:T(8,128)(2,1)S(1)}, bf16[32,12,4096]{2,0,1:T(8,128)(2,1)}, u32[]{:S(2)}) copy-start(bf16[32,12,4096]{2,0,1:T(8,128)(2,1)} %param.9) | copy-start | bytes 9437188
  13.6 2.5 %copy-start.2 = (s32[4]{0:T(128)S(1)}, s32[4]{0:T(128)}, u32[]{:S(2)}) copy-start(s32[4]{0:T(128)} %param.11) | copy-start | bytes 52

commit v2 on v1

--- a/solution.py
+++ b/solution.py
@@ -239,7 +239,7 @@
     for pair in range(segs // 16):
         base = pair * 512
         wide = jnp.concatenate(
-            [tiles[pl.ds(base, 256), :], tiles[pl.ds(base + 256, 256), :]], axis=1
+            [tiles[base : base + 256], tiles[base + 256 : base + 512]], axis=1
         )
         mixed = jnp.dot(first[...], wide, preferred_element_type=jnp.float32)
         for side in range(2):
@@ -272,9 +272,10 @@
 ):
     @pl.when(pl.program_id(0) == 0)
     def _():
-        transform(shared, None, first, second, twist, source)
-
-    transform(tiles, weight, first, second, twist, white)
+        transform(shared[...], None, first, second, twist, source)
+
+    flat = tiles[...].reshape(BLOCK * seg_count * SLOW, FAST)
+    transform(flat, weight, first, second, twist, white)
 
     def one_channel(chan, carry):
         strips = []
@@ -283,8 +284,8 @@
             real_sum = [None] * NSRC
             imag_sum = [None] * NSRC
             for seg in range(seg_count):
-                w_real = white[0, chan * seg_count + seg, rows]
-                w_imag = white[1, chan * seg_count + seg, rows]
+                w_real = white[0, seg * BLOCK + chan, rows]
+                w_imag = white[1, seg * BLOCK + chan, rows]
                 for src in range(NSRC):
                     s_real = source[0, src * seg_count + seg, rows]
                     s_imag = source[1, src * seg_count + seg, rows]
@@ -320,9 +321,42 @@
     lax.fori_loop(0, BLOCK, one_channel, 0)
 
 
-def stack(tiles, weight, shared, chan_count, seg_count, xcount, zcount, out_scale):
+def pick_kernel(src, flags, tiles, out):
+    seg_count, chan_count = tiles.shape[0], flags.shape[0] // tiles.shape[0]
+    want = src[pl.program_id(0)]
+    here = want // chan_count == lax.axis_index("chan")
+    row = want % chan_count
+    for seg in range(seg_count):
+        keep = here & (flags[seg * chan_count + row] != 0)
+        factor = jnp.where(keep, 1.0, 0.0)
+        out[0, seg] = (tiles[seg, 0].astype(jnp.float32) * factor).astype(out.dtype)
+
+
+def pick(tiled, flags, src_chan):
+    seg_count, chan_count = tiled.shape[:2]
+    return pl.pallas_call(
+        pick_kernel,
+        grid_spec=pltpu.PrefetchScalarGridSpec(
+            num_scalar_prefetch=2,
+            grid=(NSRC,),
+            in_specs=[
+                pl.BlockSpec(
+                    (seg_count, 1, SLOW, FAST),
+                    lambda i, src, flags: (0, src[i] % chan_count, 0, 0),
+                )
+            ],
+            out_specs=pl.BlockSpec(
+                (1, seg_count, SLOW, FAST), lambda i, src, flags: (i, 0, 0, 0)
+            ),
+        ),
+        out_shape=jax.ShapeDtypeStruct((NSRC, seg_count, SLOW, FAST), tiled.dtype),
+        name="pick",
+    )(src_chan, flags, tiled)
+
+
+def stack(tiles, weight, shared, xcount, zcount, out_scale):
+    seg_count, chan_count = tiles.shape[:2]
     per = chan_count // (xcount * zcount)
-    block_rows = BLOCK * seg_count * SLOW
     consts = tables(out_scale)
     turns = xcount // 2
 
@@ -335,7 +369,7 @@
         grid=(chan_count // BLOCK,),
         out_shape=jax.ShapeDtypeStruct((xcount, zcount, per, NSRC, SLOW, FAST), jnp.bfloat16),
         in_specs=[
-            pl.BlockSpec((block_rows, FAST), lambda i: (i, 0)),
+            pl.BlockSpec((seg_count, BLOCK, SLOW, FAST), lambda i: (0, i, 0, 0)),
             pl.BlockSpec((BLOCK * seg_count, FAST), lambda i: (i, 0)),
             whole(shared),
         ]
@@ -360,31 +394,15 @@
     xcount = 4
     zcount = group_count // xcount
     ycount = lax.axis_size("chan") // 4
-    tiled = recordings.reshape(chan_count, seg_count, SLOW, FAST)
-    src_owner = src_chan // chan_count
-    src_row = src_chan % chan_count
     out_scale = 1.0 / math.sqrt(samples * seg_count * group_count)
-    mine = []
-    for source in range(NSRC):
-        own = lax.dynamic_index_in_dim(tiled, src_row[source], 0, keepdims=False)
-        flags = lax.dynamic_index_in_dim(valid_mask, src_row[source], 0, keepdims=False)
-        here = (flags != 0) & (lax.axis_index("chan") == src_owner[source])
-        mine.append(jnp.where(here[:, None, None], own, jnp.zeros_like(own)))
-    shared = share(jnp.stack(mine).reshape(NSRC * seg_count * SLOW, FAST), ycount)
-    weight = jnp.broadcast_to(
-        valid_mask.astype(jnp.float32).reshape(chan_count * seg_count, 1),
-        (chan_count * seg_count, FAST),
-    )
-    parts = stack(
-        tiled.reshape(chan_count * seg_count * SLOW, FAST),
-        weight,
-        shared,
-        chan_count,
-        seg_count,
-        xcount,
-        zcount,
-        out_scale,
-    )
+    tiled = jnp.transpose(recordings, (1, 0, 2)).reshape(seg_count, chan_count, SLOW, FAST)
+    flags = jnp.transpose(valid_mask)
+    mine = pick(tiled, flags.reshape(-1), src_chan)
+    shared = share(mine.reshape(NSRC * seg_count * SLOW, FAST), ycount)
+    weight = flags.astype(jnp.float32).reshape(seg_count, chan_count // BLOCK, BLOCK)
+    weight = jnp.transpose(weight, (1, 0, 2)).reshape(chan_count * seg_count, 1)
+    weight = jnp.broadcast_to(weight, (chan_count * seg_count, FAST))
+    parts = stack(tiled, weight, shared, xcount, zcount, out_scale)
     summed = gather(parts)
     return jnp.transpose(summed, (1, 0, 2, 3)).reshape(NSRC, chan_count // group_count, samples)
 

time: 126 us -> 108 us (0.86)
  between operations: 10.2 us -> 0.03 us
  local copies, waits for them, and re-layouts: 18.5 us -> 9.29 us
  Pallas kernels: 94 us -> 97.9 us
  other arithmetic: 2.21 us -> 0.01 us
    another operation x1 -> x0, local copies, waits for them, and re-layouts: 6.96 us -> none  [per_device(): tiled.reshape(chan_count * seg_count * SLOW, FAST)]
    pallas_call x0 -> x1, Pallas kernels: none -> 3.84 us  [pick(): pl.pallas_call(pick_kernel, grid_spec=pltpu.PrefetchScalarGridSpec(num_sc...]
    unnamed x8 -> x2, local copies, waits for them, and re-layouts: 8.15 us -> 5.18 us
    reshape x0 -> x1, local copies, waits for them, and re-layouts: none -> 1.35 us  [per_device(): mine = pick(tiled, flags.reshape(-1), src_chan)]
where the time goes in v2:
time: 108 us; the launch traced here: 107 us
  Pallas kernels  97.9 us (91%)
  local copies, waits for them, and re-layouts  9.29 us (9%)
    pallas_call x1, Pallas kernels, share(): pl.pallas_call(functools.partial(share_kernel, ycount), out_shape=jax.Sha...  37.1 us
    pallas_call x1, Pallas kernels, stack(): pl.pallas_call(functools.partial(stack_kernel, seg_count), grid=(chan_cou...  31.3 us
    pallas_call x1, Pallas kernels, gather(): pl.pallas_call(functools.partial(gather_kernel, xcount, zcount), out_shap...  25.6 us
    unnamed x2, local copies, waits for them, and re-layouts  5.18 us
    pallas_call x1, Pallas kernels, pick(): pl.pallas_call(pick_kernel, grid_spec=pltpu.PrefetchScalarGridSpec(num_sc...  3.84 us

profile of v2, /device:TPU:1, one launch (start us, length us, event | category | flops | bytes accessed | tf_op | source)
XLA Modules:
  0.0 107.3 jit_solution(13463479614908876257)
XLA Ops:
  0.0 1.4 %reshape.19.flags = s32[384]{0:T(512)} reshape(s32[12,32]{1,0:T(8,128)} %bitcast.25) | data formatting | bytes 3072 | tf_op jit(solution)/shard_map/reshape | solution.py:400
  1.4 0.8 copy.14
  2.1 0.1 copy.15
  2.3 0.1 broadcast_in_dim.7
  2.4 0.8 broadcast_in_dim.8.weight
  3.2 4.4 %copy.19 = bf16[48,8,32,128]{3,2,1,0:T(8,128)(2,1)} copy(bf16[48,8,32,128]{3,1,2,0:T(8,128)(2,1)} %bitcast.20) | data formatting | bytes 6291456
  7.6 3.8 %pick.1 = bf16[4,12,32,128]{3,2,1,0:T(8,128)(2,1)} custom-call(s32[4]{0:T(128)} %src.1, s32[384]{0:T(512)} %reshape.19.flags, bf16[12,32,32,128]{3,2,1,0:T(8,128)(2,1)} %bitcast.18), custom_call_target="tpu_custom_call" | custom-call | tf_op jit(solution)/shard_map/pick/pallas_call | solution.py:337
  11.4 37.1 %share.1 = bf16[2,8,96,128]{3,2,1,0:T(8,128)(2,1)} custom-call(bf16[2,8,96,128]{3,2,1,0:T(8,128)(2,1)} %bitcast.21), custom_call_target="tpu_custom_call" | custom-call | tf_op jit(solution)/shard_map/share/pallas_call | solution.py:134
  48.6 31.3 %stack.1.parts = bf16[4,4,2,4,32,128]{5,4,3,2,1,0:T(8,128)(2,1)} custom-call(bf16[12,32,32,128]{3,2,1,0:T(8,128)(2,1)} %bitcast.19, f32[384,128]{1,0:T(8,128)} %broadcast_in_dim.8.weight, bf16[1536,128]{1,0:T(8,128)(2,1)} %bitcast.22, bf16[512,256]{1,0:T(8,128)(2,1)} %constant.12.clone.first, bf16[256,256]{1,0:T(8,128)(2,1)} %constant.13.clone.second, ...), custom_call_target="tpu_custom_call" | custom-call | tf_op jit(solution)/shard_map/stack/pallas_call | solution.py:367
  79.9 25.6 %gather.1 = f32[2,4,32,128]{3,2,1,0:T(8,128)} custom-call(bf16[4,4,2,4,32,128]{5,4,3,2,1,0:T(8,128)(2,1)} %stack.1.parts), custom_call_target="tpu_custom_call" | custom-call | tf_op jit(solution)/shard_map/gather/pallas_call | solution.py:215
  105.5 0.9 reshape.21
  106.5 0.8 copy.17
  (1 shorter events, 0.0 us)

commit v3 on v0

v3 whole, which is shorter than its diff:
```python
import functools
import math

import jax
import jax.numpy as jnp
import numpy as np
from jax import lax
from jax.experimental import pallas as pl
from jax.experimental.pallas import tpu as pltpu
from jax.sharding import PartitionSpec as P

NSRC = 4
SLOW = 32
FAST = 128
BLOCK = 4
MESH = pl.DeviceIdType.MESH
VMEM_LIMIT = 60 * 1024 * 1024


def angles(rows_count, cols_count, period):
    left_index = np.arange(rows_count)[:, None]
    right_index = np.arange(cols_count)[None, :]
    return 2.0 * math.pi / period * (left_index * right_index % period)


def tables(out_scale):
    slow = angles(SLOW, SLOW, SLOW)
    fast = angles(FAST, FAST, FAST)
    twist = angles(SLOW, FAST, SLOW * FAST)
    first = np.kron(np.eye(8), np.concatenate([np.cos(slow), -np.sin(slow)], axis=0))
    second = np.block([[np.cos(fast), -np.sin(fast)], [np.sin(fast), np.cos(fast)]])
    back = np.block([[np.cos(fast), np.sin(fast)], [-np.sin(fast), np.cos(fast)]])
    outer = np.concatenate(
        [np.kron(np.eye(NSRC), np.cos(slow)), np.kron(np.eye(NSRC), -np.sin(slow))], axis=1
    )
    return (
        jnp.asarray(first, jnp.bfloat16),
        jnp.asarray(second, jnp.bfloat16),
        jnp.asarray(back, jnp.bfloat16),
        jnp.asarray(outer, jnp.bfloat16),
        jnp.asarray(np.stack([np.cos(twist), np.sin(twist)]), jnp.float32),
        jnp.asarray(np.stack([np.cos(twist), np.sin(twist)]) * out_scale, jnp.float32),
    )


def exchange(source, target, send, recv, device):
    return pltpu.make_async_remote_copy(
        src_ref=source,
        dst_ref=target,
        send_sem=send,
        recv_sem=recv,
        device_id=device,
        device_id_type=MESH,
    )


def greet(devices):
    barrier = pltpu.get_barrier_semaphore()
    for device in devices:
        pl.semaphore_signal(barrier, inc=1, device_id=device, device_id_type=MESH)
    pl.semaphore_wait(barrier, len(devices))


def transform(tiles, weight, first, second, twist, store):
    lane = lax.broadcasted_iota(jnp.int32, (8, FAST), 1)
    for pair in range(tiles.shape[0] // 512):
        base = pair * 512
        wide = jnp.concatenate(
            [tiles[base : base + 256], tiles[base + 256 : base + 512]], axis=1
        )
        mixed = jnp.dot(first[...], wide, preferred_element_type=jnp.float32)
        for side in range(2):
            group = mixed[:, side * FAST : (side + 1) * FAST].reshape(8, 2 * SLOW, FAST)
            real_part = group[:, :SLOW]
            imag_part = group[:, SLOW:]
            twist_cos = twist[0][None]
            twist_sin = twist[1][None]
            z_real = (real_part * twist_cos + imag_part * twist_sin).astype(jnp.bfloat16)
            z_imag = (imag_part * twist_cos - real_part * twist_sin).astype(jnp.bfloat16)
            joined = jnp.concatenate([z_real, z_imag], axis=2).reshape(8 * SLOW, 2 * FAST)
            bins = jnp.dot(joined, second[...], preferred_element_type=jnp.float32)
            x_real = bins[:, :FAST].reshape(8, SLOW, FAST)
            x_imag = bins[:, FAST:].reshape(8, SLOW, FAST)
            power = jnp.sum(x_real * x_real + x_imag * x_imag, axis=1)
            other = jnp.where(
                lane % 2 == 0, pltpu.roll(power, FAST - 1, 1), pltpu.roll(power, 1, 1)
            )
            scale = lax.rsqrt((power + other) * (1.0 / (2 * SLOW)) + 1e-06)
            at = pair * 16 + side * 8
            if weight is not None:
                scale = scale * weight(at)
            scale = scale[:, None, :]
            store(
                at,
                (x_real * scale).astype(jnp.bfloat16).astype(jnp.float32),
                (x_imag * scale).astype(jnp.bfloat16).astype(jnp.float32),
            )


def whole_kernel(
    ycount, xcount, zcount,
    own, tiles, flags, eye, first, second, back, outer, twist, turn,
    out,
    white, source, weights,
    pair_in, half, slices_in, part, across_in, whole, twin,
    parts, x_in, mid, z_in,
    s1, r1, s2, r2, s3, r3, s4, r4, s5, r5, s6, r6, s7, r7,
):
    seg_count, chan_count = tiles.shape[:2]
    segs = seg_count * BLOCK
    me = lax.axis_index("chan")
    core = me % 2
    y = me // 2 % ycount
    z = me // (2 * ycount)
    sibling = {"chan": me - core + (1 - core)}
    opposite = {"chan": ((1 - z) * ycount + y) * 2 + core}
    spot = lax.axis_index("tm")
    sx = spot % xcount
    sz = spot // xcount

    def along(step):
        return (y + step) % ycount

    def at_y(place):
        return {"chan": (z * ycount + place) * 2 + core}

    def at_xz(zpos, xpos):
        return {"tm": zpos * xcount + xpos}

    greet(
        [sibling, opposite]
        + [at_y(along(step)) for step in range(1, ycount)]
        + [at_xz(sz, (sx + step) % xcount) for step in range(1, xcount)]
        + [at_xz((sz + step) % zcount, sx) for step in range(1, zcount)]
    )

    def forward(low, high):
        def one_block(block, carry):
            flat = tiles[:, pl.ds(block * BLOCK, BLOCK)].reshape(segs * SLOW, FAST)

            def weight(at):
                return weights[block, at : at + 8]

            def store(at, real, imag):
                white[0, block, at : at + 8] = real
                white[1, block, at : at + 8] = imag

            transform(flat, weight, first, second, twist, store)
            return carry

        lax.fori_loop(low, high, one_block, 0)

    copy = exchange(own.at[1 - core], pair_in, s1, r1, sibling)
    copy.start()
    spread = (flags[...].astype(jnp.float32)[:, None, :] * eye[...][None]).astype(jnp.bfloat16)
    rows = jnp.dot(
        spread.reshape(seg_count * chan_count, chan_count),
        jnp.ones((chan_count, FAST), jnp.bfloat16),
        preferred_element_type=jnp.float32,
    ).reshape(seg_count, chan_count, FAST)
    for block in range(chan_count // BLOCK):
        weights[block] = rows[:, block * BLOCK : (block + 1) * BLOCK].reshape(segs, FAST)
    forward(0, 1)
    copy.wait()
    half[...] = own[core] + pair_in[...]

    copies = []
    for step in range(1, ycount):
        to = along(step)
        copies.append(
            exchange(half.at[to], slices_in.at[step - 1], s2.at[step - 1], r2.at[step - 1], at_y(to))
        )
        copies[-1].start()
    forward(1, 3)
    for copy in copies:
        copy.wait()
    total = half[y]
    for step in range(ycount - 1):
        total = total + slices_in[step]
    part[...] = total

    copy = exchange(part, across_in, s3, r3, opposite)
    copy.start()
    forward(3, 5)
    copy.wait()
    whole[y] = part[...] + across_in[...]

    copies = []
    for step in range(1, ycount):
        copies.append(
            exchange(
                whole.at[y], whole.at[y], s4.at[step - 1], r4.at[step - 1], at_y(along(step))
            )
        )
        copies[-1].start()
    forward(5, 7)
    for copy in copies:
        copy.wait()

    copy = exchange(whole, twin, s5, r5, sibling)
    copy.start()
    forward(7, chan_count // BLOCK)
    copy.wait()

    low = jnp.where(core == 0, whole[...], twin[...]).reshape(segs * SLOW // 2, FAST)
    high = jnp.where(core == 0, twin[...], whole[...]).reshape(segs * SLOW // 2, FAST)

    def store_source(at, real, imag):
        for seg in range(8):
            src, place = (at + seg) // seg_count, (at + seg) % seg_count
            source[0, place, src] = real[seg]
            source[1, place, src] = imag[seg]

    transform(jnp.concatenate([low, high], axis=0), None, first, second, twist, store_source)

    def one_channel(block, lead, target):
        real_rows, imag_rows = [], []
        for strip in range(SLOW // 16):
            rows = slice(strip * 16, strip * 16 + 16)
            real_sum = imag_sum = None
            for seg in range(seg_count):
                w_real = white[0, block, seg * BLOCK + lead, rows][None]
                w_imag = white[1, block, seg * BLOCK + lead, rows][None]
                s_real = source[0, seg, :, rows]
                s_imag = source[1, seg, :, rows]
                real_now = s_real * w_real + s_imag * w_imag
                imag_now = s_real * w_imag - s_imag * w_real
                real_sum = real_now if seg == 0 else real_sum + real_now
                imag_sum = imag_now if seg == 0 else imag_sum + imag_now
            real_rows.append(real_sum.astype(jnp.bfloat16))
            imag_rows.append(imag_sum.astype(jnp.bfloat16))
        both = jnp.concatenate(
            [jnp.concatenate(real_rows, axis=1), jnp.concatenate(imag_rows, axis=1)], axis=2
        ).reshape(NSRC * SLOW, 2 * FAST)
        v = jnp.dot(both, back[...], preferred_element_type=jnp.float32)
        v_real = v[:, :FAST].reshape(NSRC, SLOW, FAST)
        v_imag = v[:, FAST:].reshape(NSRC, SLOW, FAST)
        turn_cos = turn[0][None]
        turn_sin = turn[1][None]
        w_real = (v_real * turn_cos - v_imag * turn_sin).astype(jnp.bfloat16)
        w_imag = (v_real * turn_sin + v_imag * turn_cos).astype(jnp.bfloat16)
        tall = jnp.concatenate(
            [w_real.reshape(NSRC * SLOW, FAST), w_imag.reshape(NSRC * SLOW, FAST)], axis=0
        )
        lagged = jnp.dot(outer[...], tall, preferred_element_type=jnp.float32)
        target[...] = lagged.astype(jnp.bfloat16).reshape(NSRC, SLOW, FAST)

    per = parts.shape[2]

    def one_group(to):
        def one(index, carry):
            place = index // per
            which = index % per
            chan = per * (place * xcount + to) + which
            one_channel(chan // BLOCK, chan % BLOCK, parts.at[to, place, which])
            return carry

        lax.fori_loop(0, zcount * per, one, 0)

    copies = []
    for step in range(1, xcount):
        to = (sx + step) % xcount
        one_group(to)
        copies.append(
            exchange(parts.at[to], x_in.at[step - 1], s6.at[step - 1], r6.at[step - 1], at_xz(sz, to))
        )
        copies[-1].start()
    one_group(sx)
    for copy in copies:
        copy.wait()

    def add_up(place):
        total = parts[sx, place].astype(jnp.float32)
        for step in range(xcount - 1):
            total = total + x_in[step, place].astype(jnp.float32)
        return total

    copies = []
    for step in range(1, zcount):
        to = (sz + step) % zcount
        mid[step - 1] = add_up(to).astype(jnp.bfloat16)
        copies.append(
            exchange(mid.at[step - 1], z_in.at[step - 1], s7.at[step - 1], r7.at[step - 1], at_xz(to, sx))
        )
        copies[-1].start()
    total = add_up(sz)
    for copy in copies:
        copy.wait()
    for step in range(zcount - 1):
        total = total + z_in[step].astype(jnp.float32)
    out[...] = total


def process(own, tiles, flags, ycount, xcount, zcount, out_scale):
    seg_count, chan_count = tiles.shape[:2]
    per = chan_count // (xcount * zcount)
    rows = NSRC * seg_count * SLOW
    slab = rows // (2 * ycount)
    dtype = own.dtype
    shaped = own.reshape(2, ycount, slab, FAST)
    half = (ycount, slab, FAST)
    result = (per, NSRC, SLOW, FAST)
    dma = pltpu.SemaphoreType.DMA
    vmem = pltpu.VMEM
    spec = pl.BlockSpec(memory_space=pltpu.VMEM)
    operands = (shaped, tiles, flags, jnp.eye(chan_count, dtype=jnp.float32)) + tables(out_scale)
    return pl.pallas_call(
        functools.partial(whole_kernel, ycount, xcount, zcount),
        out_shape=jax.ShapeDtypeStruct(result, jnp.float32),
        in_specs=[spec] * len(operands),
        out_specs=spec,
        scratch_shapes=[
            vmem((2, chan_count // BLOCK, BLOCK * seg_count, SLOW, FAST), jnp.float32),
            vmem((2, seg_count, NSRC, SLOW, FAST), jnp.float32),
            vmem((chan_count // BLOCK, BLOCK * seg_count, FAST), jnp.float32),
            vmem(half, dtype),
            vmem(half, dtype),
            vmem((ycount - 1, slab, FAST), dtype),
            vmem((slab, FAST), dtype),
            vmem((slab, FAST), dtype),
            vmem(half, dtype),
            vmem(half, dtype),
            vmem((xcount, zcount) + result, dtype),
            vmem((xcount - 1, zcount) + result, dtype),
            vmem((zcount - 1,) + result, dtype),
            vmem((zcount - 1,) + result, dtype),
            dma,
            dma,
            dma((ycount - 1,)),
            dma((ycount - 1,)),
            dma,
            dma,
            dma((ycount - 1,)),
            dma((ycount - 1,)),
            dma,
            dma,
            dma((xcount - 1,)),
            dma((xcount - 1,)),
            dma((zcount - 1,)),
            dma((zcount - 1,)),
        ],
        compiler_params=pltpu.CompilerParams(
            collective_id=0, has_side_effects=True, vmem_limit_bytes=VMEM_LIMIT
        ),
        name="process",
    )(*operands)


def pick_kernel(src, flags, tiles, out):
    seg_count, chan_count = tiles.shape[0], flags.shape[1]
    want = src[pl.program_id(0)]
    here = want // chan_count == lax.axis_index("chan")
    row = want % chan_count
    for seg in range(seg_count):
        keep = here & (flags[seg, row] != 0)
        factor = jnp.where(keep, 1.0, 0.0)
        out[0, seg] = (tiles[seg, 0].astype(jnp.float32) * factor).astype(out.dtype)


def pick(tiled, flags, src_chan):
    seg_count, chan_count = tiled.shape[:2]
    return pl.pallas_call(
        pick_kernel,
        grid_spec=pltpu.PrefetchScalarGridSpec(
            num_scalar_prefetch=2,
            grid=(NSRC,),
            in_specs=[
                pl.BlockSpec(
                    (seg_count, 1, SLOW, FAST),
                    lambda i, src, flags: (0, src[i] % chan_count, 0, 0),
                )
            ],
            out_specs=pl.BlockSpec(
                (1, seg_count, SLOW, FAST), lambda i, src, flags: (i, 0, 0, 0)
            ),
        ),
        out_shape=jax.ShapeDtypeStruct((NSRC, seg_count, SLOW, FAST), tiled.dtype),
        name="pick",
    )(src_chan, flags, tiled)


def per_device(recordings, valid_mask, src_chan):
    chan_count, seg_count, samples = recordings.shape
    group_count = lax.axis_size("tm")
    xcount = 4
    zcount = group_count // xcount
    ycount = lax.axis_size("chan") // 4
    out_scale = 1.0 / math.sqrt(samples * seg_count * group_count)
    tiled = jnp.transpose(recordings, (1, 0, 2)).reshape(seg_count, chan_count, SLOW, FAST)
    flags = jnp.transpose(valid_mask)
    mine = pick(tiled, flags, src_chan)
    summed = process(mine, tiled, flags, ycount, xcount, zcount, out_scale)
    return jnp.transpose(summed, (1, 0, 2, 3)).reshape(NSRC, chan_count // group_count, samples)


def solution(mesh):
    return jax.shard_map(
        per_device,
        mesh=mesh,
        in_specs=(P("chan", "tm", None), P("chan", "tm"), P()),
        out_specs=P(None, ("chan", "tm"), None),
        check_vma=False,
    )
```

time: 557 us -> 81 us (0.15)
  the two profiles are of different devices: /device:TPU:57 before, /device:TPU:2 now
where the time goes in v3:
time: 81 us; the launch traced here: 80.7 us
  Pallas kernels  73.9 us (91%)
  local copies, waits for them, and re-layouts  6.11 us (8%)
    pallas_call x1, Pallas kernels, process(): pl.pallas_call(functools.partial(whole_kernel, ycount, xcount, zcount), o...  70 us
    unnamed x1, local copies, waits for them, and re-layouts  4.4 us
    pallas_call x1, Pallas kernels, pick(): pl.pallas_call(pick_kernel, grid_spec=pltpu.PrefetchScalarGridSpec(num_sc...  3.95 us
    reshape x2, local copies, waits for them, and re-layouts, per_device(): jnp.transpose(summed, (1, 0, 2, 3))  1.71 us

profile of v3, /device:TPU:2, one launch (start us, length us, event | category | flops | bytes accessed | tf_op | source)
XLA Modules:
  0.0 80.7 jit_solution(16568947416539309087)
XLA Ops:
  0.0 0.6 fusion.eye
  0.6 4.4 %copy.11 = bf16[48,8,32,128]{3,2,1,0:T(8,128)(2,1)} copy(bf16[48,8,32,128]{3,1,2,0:T(8,128)(2,1)} %bitcast.14) | data formatting | bytes 6291456
  5.0 4.0 %pick.1 = bf16[4,12,32,128]{3,2,1,0:T(8,128)(2,1)} custom-call(s32[4]{0:T(128)} %src.1, s32[12,32]{1,0:T(8,128)} %bitcast.17, bf16[12,32,32,128]{3,2,1,0:T(8,128)(2,1)} %bitcast.12), custom_call_target="tpu_custom_call" | custom-call | tf_op jit(solution)/shard_map/pick/pallas_call | solution.py:362
  9.0 70.0 %process.1 = f32[2,4,32,128]{3,2,1,0:T(8,128)} custom-call(bf16[2,8,96,128]{3,2,1,0:T(8,128)(2,1)} %bitcast.15, bf16[12,32,32,128]{3,2,1,0:T(8,128)(2,1)} %bitcast.13, s32[12,32]{1,0:T(8,128)} %bitcast.18, f32[32,32]{1,0:T(8,128)} %fusion.eye, bf16[512,256]{1,0:T(8,128)(2,1)} %constant.12.clone.first, bf16[256,256]{1,0:T(8,128)(2,1)} %constant.13.clone.second, ...), custom_call_target="tpu_custom_call" | custom-call | tf_op jit(solution)/shard_map/process/pallas_call | solution.py:307
  79.0 0.9 %reshape.11 = f32[4,2,4096]{2,0,1:T(4,128)S(1)} reshape(f32[4,2,32,128]{3,2,0,1:T(8,128)} %bitcast.16) | data formatting | bytes 262144 | tf_op jit(solution)/shard_map/reshape | solution.py:393
  79.9 0.8 copy.10

commit v4 on v3

v4 whole, which is shorter than its diff:
```python
import functools
import math

import jax
import jax.numpy as jnp
import numpy as np
from jax import lax
from jax.experimental import pallas as pl
from jax.experimental.pallas import tpu as pltpu
from jax.sharding import PartitionSpec as P

NSRC = 4
SLOW = 32
FAST = 128
BLOCK = 6
MESH = pl.DeviceIdType.MESH
VMEM_LIMIT = 60 * 1024 * 1024


def angles(rows_count, cols_count, period):
    left_index = np.arange(rows_count)[:, None]
    right_index = np.arange(cols_count)[None, :]
    return 2.0 * math.pi / period * (left_index * right_index % period)


def tables(out_scale):
    slow = angles(SLOW, SLOW, SLOW)
    fast = angles(FAST, FAST, FAST)
    twist = angles(SLOW, FAST, SLOW * FAST)
    first = np.kron(np.eye(8), np.concatenate([np.cos(slow), -np.sin(slow)], axis=0))
    second = np.block([[np.cos(fast), -np.sin(fast)], [np.sin(fast), np.cos(fast)]])
    back = np.block([[np.cos(fast), np.sin(fast)], [-np.sin(fast), np.cos(fast)]])
    outer = np.concatenate(
        [np.kron(np.eye(NSRC), np.cos(slow)), np.kron(np.eye(NSRC), -np.sin(slow))], axis=1
    )
    return (
        jnp.asarray(first, jnp.bfloat16),
        jnp.asarray(
            first.reshape(-1, 8, SLOW).transpose(0, 2, 1).reshape(first.shape), jnp.bfloat16
        ),
        jnp.asarray(second, jnp.bfloat16),
        jnp.asarray(back, jnp.bfloat16),
        jnp.asarray(outer, jnp.bfloat16),
        jnp.asarray(np.stack([np.cos(twist), np.sin(twist)]), jnp.float32),
        jnp.asarray(np.stack([np.cos(twist), np.sin(twist)]) * out_scale, jnp.float32),
    )


def exchange(source, target, send, recv, device):
    return pltpu.make_async_remote_copy(
        src_ref=source,
        dst_ref=target,
        send_sem=send,
        recv_sem=recv,
        device_id=device,
        device_id_type=MESH,
    )


def greet(devices):
    barrier = pltpu.get_barrier_semaphore()
    for device in devices:
        pl.semaphore_signal(barrier, inc=1, device_id=device, device_id_type=MESH)
    return barrier, len(devices)


def transform(tiles, weight, first, second, twist, store):
    lane = lax.broadcasted_iota(jnp.int32, (8, FAST), 1)
    for pair in range(tiles.shape[0] // 2):
        wide = jnp.concatenate([tiles[2 * pair], tiles[2 * pair + 1]], axis=1)
        mixed = jnp.dot(first[...], wide, preferred_element_type=jnp.float32)
        for side in range(2):
            group = mixed[:, side * FAST : (side + 1) * FAST].reshape(8, 2 * SLOW, FAST)
            real_part = group[:, :SLOW]
            imag_part = group[:, SLOW:]
            twist_cos = twist[0][None]
            twist_sin = twist[1][None]
            z_real = (real_part * twist_cos + imag_part * twist_sin).astype(jnp.bfloat16)
            z_imag = (imag_part * twist_cos - real_part * twist_sin).astype(jnp.bfloat16)
            joined = jnp.concatenate([z_real, z_imag], axis=2).reshape(8 * SLOW, 2 * FAST)
            bins = jnp.dot(joined, second[...], preferred_element_type=jnp.float32)
            x_real = bins[:, :FAST].reshape(8, SLOW, FAST)
            x_imag = bins[:, FAST:].reshape(8, SLOW, FAST)
            power = jnp.sum(x_real * x_real + x_imag * x_imag, axis=1)
            other = jnp.where(
                lane % 2 == 0, pltpu.roll(power, FAST - 1, 1), pltpu.roll(power, 1, 1)
            )
            scale = lax.rsqrt((power + other) * (1.0 / (2 * SLOW)) + 1e-06)
            at = pair * 2 + side
            if weight is not None:
                scale = scale * weight(at)
            scale = scale[:, None, :]
            store(
                at,
                (x_real * scale).astype(jnp.bfloat16).astype(jnp.float32),
                (x_imag * scale).astype(jnp.bfloat16).astype(jnp.float32),
            )


def whole_kernel(
    ycount, xcount, zcount,
    src, marks, tiles, flags, eye, first, first_by_n, second, back, outer, twist, turn,
    out,
    white, source, weights, own,
    pair_in, half, slices_in, part, across_in, whole, twin,
    parts, x_in, mid, z_in,
    s1, r1, s2, r2, s3, r3, s4, r4, s5, r5, s6, r6, s7, r7,
):
    seg_count, chan_count = flags.shape
    sets = chan_count // 8
    me = lax.axis_index("chan")
    core = me % 2
    y = me // 2 % ycount
    z = me // (2 * ycount)
    sibling = {"chan": me - core + (1 - core)}
    opposite = {"chan": ((1 - z) * ycount + y) * 2 + core}
    spot = lax.axis_index("tm")
    sx = spot % xcount
    sz = spot // xcount

    def along(step):
        return (y + step) % ycount

    def at_y(place):
        return {"chan": (z * ycount + place) * 2 + core}

    def at_xz(zpos, xpos):
        return {"tm": zpos * xcount + xpos}

    barrier, count = greet(
        [sibling, opposite]
        + [at_y(along(step)) for step in range(1, ycount)]
        + [at_xz(sz, (sx + step) % xcount) for step in range(1, xcount)]
        + [at_xz((sz + step) % zcount, sx) for step in range(1, zcount)]
    )

    def forward(low, high):
        def one_block(block, carry):
            start = block * BLOCK

            def weight(at):
                return weights[start + at]

            def store(at, real, imag):
                seg = (start + at) // sets
                chan = (start + at) % sets * 8
                white[0, seg, pl.ds(chan, 8)] = real
                white[1, seg, pl.ds(chan, 8)] = imag

            transform(tiles[pl.ds(start, BLOCK)], weight, first_by_n, second, twist, store)
            return carry

        lax.fori_loop(low, high, one_block, 0)

    slot = lax.broadcasted_iota(jnp.int32, (SLOW, 8 * SLOW), 1)
    line = lax.broadcasted_iota(jnp.int32, (SLOW, 8 * SLOW), 0) * 8
    for index in range(NSRC):
        want = src[index]
        here = jnp.where(want // chan_count == me, 1, 0)
        row = want % chan_count
        chosen = jnp.where(slot == line + row % 8, 1.0, 0.0).astype(jnp.bfloat16)
        for seg in range(0, seg_count, 2):
            wide = jnp.concatenate(
                [tiles[seg * sets + row // 8], tiles[(seg + 1) * sets + row // 8]], axis=1
            )
            found = jnp.dot(chosen, wide, preferred_element_type=jnp.float32)
            for side in range(2):
                factor = (here * marks[seg + side, row]).astype(jnp.float32)
                place = (index % 2) * seg_count + seg + side
                per_slab = own.shape[2]
                own[index // 2, place // per_slab, place % per_slab] = (
                    found[:, side * FAST : (side + 1) * FAST] * factor
                ).astype(jnp.bfloat16)

    pl.semaphore_wait(barrier, count)
    copy = exchange(own.at[1 - core], pair_in, s1, r1, sibling)
    copy.start()
    spread = (flags[...].astype(jnp.float32)[:, None, :] * eye[...][None]).astype(jnp.bfloat16)
    rows = jnp.dot(
        spread.reshape(seg_count * chan_count, chan_count),
        jnp.ones((chan_count, FAST), jnp.bfloat16),
        preferred_element_type=jnp.float32,
    ).reshape(seg_count, chan_count, FAST)
    weights[...] = rows.reshape(seg_count * sets, 8, FAST)
    forward(0, 1)
    copy.wait()
    half[...] = own[core] + pair_in[...]

    copies = []
    for step in range(1, ycount):
        to = along(step)
        copies.append(
            exchange(half.at[to], slices_in.at[step - 1], s2.at[step - 1], r2.at[step - 1], at_y(to))
        )
        copies[-1].start()
    forward(1, 3)
    for copy in copies:
        copy.wait()
    total = half[y]
    for step in range(ycount - 1):
        total = total + slices_in[step]
    part[...] = total

    copy = exchange(part, across_in, s3, r3, opposite)
    copy.start()
    forward(3, 5)
    copy.wait()
    whole[y] = part[...] + across_in[...]

    copies = []
    for step in range(1, ycount):
        copies.append(
            exchange(
                whole.at[y], whole.at[y], s4.at[step - 1], r4.at[step - 1], at_y(along(step))
            )
        )
        copies[-1].start()
    forward(5, 7)
    for copy in copies:
        copy.wait()

    copy = exchange(whole, twin, s5, r5, sibling)
    copy.start()
    forward(7, seg_count * sets // BLOCK)
    copy.wait()

    low = jnp.where(core == 0, whole[...], twin[...])
    high = jnp.where(core == 0, twin[...], whole[...])

    def store_source(at, real, imag):
        for seg in range(8):
            index, place = (at * 8 + seg) // seg_count, (at * 8 + seg) % seg_count
            source[0, place, index] = real[seg]
            source[1, place, index] = real[seg] - imag[seg]
            source[2, place, index] = real[seg] + imag[seg]

    both_halves = jnp.concatenate([low, high], axis=0).reshape(-1, 8 * SLOW, FAST)
    transform(both_halves, None, first, second, twist, store_source)

    per = parts.shape[2]

    def some_channels(chan, to, place):
        real_rows = [[] for _ in range(per)]
        imag_rows = [[] for _ in range(per)]
        for strip in range(SLOW // 8):
            rows = slice(strip * 8, strip * 8 + 8)
            sums = [[None] * 3 for _ in range(per)]
            for seg in range(seg_count):
                terms = [source[k, seg, :, rows] for k in range(3)]
                for which in range(per):
                    w_real = white[0, seg, chan + which, rows]
                    w_imag = white[1, seg, chan + which, rows]
                    for k, factor in enumerate((w_real + w_imag, w_imag, w_real)):
                        now = terms[k] * factor[None]
                        sums[which][k] = now if seg == 0 else sums[which][k] + now
            for which in range(per):
                real_rows[which].append(sums[which][0] - sums[which][1])
                imag_rows[which].append(sums[which][0] - sums[which][2])
        both = jnp.concatenate(
            [
                jnp.concatenate(
                    [
                        jnp.concatenate(real_rows[which], axis=1).astype(jnp.bfloat16),
                        jnp.concatenate(imag_rows[which], axis=1).astype(jnp.bfloat16),
                    ],
                    axis=2,
                ).reshape(NSRC * SLOW, 2 * FAST)
                for which in range(per)
            ],
            axis=0,
        )
        v = jnp.dot(both, back[...], preferred_element_type=jnp.float32)
        v_real = v[:, :FAST].reshape(per * NSRC, SLOW, FAST)
        v_imag = v[:, FAST:].reshape(per * NSRC, SLOW, FAST)
        turn_cos = turn[0][None]
        turn_sin = turn[1][None]
        w_real = (v_real * turn_cos - v_imag * turn_sin).astype(jnp.bfloat16)
        w_imag = (v_real * turn_sin + v_imag * turn_cos).astype(jnp.bfloat16)
        w_real = w_real.reshape(per, NSRC * SLOW, FAST)
        w_imag = w_imag.reshape(per, NSRC * SLOW, FAST)
        tall = jnp.concatenate(
            [
                jnp.concatenate([w_real[which], w_imag[which]], axis=0)
                for which in range(per)
            ],
            axis=1,
        )
        lagged = jnp.dot(outer[...], tall, preferred_element_type=jnp.float32)
        for which in range(per):
            parts[to, place, which] = (
                lagged[:, which * FAST : (which + 1) * FAST]
                .astype(jnp.bfloat16)
                .reshape(NSRC, SLOW, FAST)
            )

    def one_group(to):
        def one(place, carry):
            some_channels(per * (place * xcount + to), to, place)
            return carry

        lax.fori_loop(0, zcount, one, 0)

    copies = []
    for step in range(1, xcount):
        to = (sx + step) % xcount
        one_group(to)
        copies.append(
            exchange(parts.at[to], x_in.at[step - 1], s6.at[step - 1], r6.at[step - 1], at_xz(sz, to))
        )
        copies[-1].start()
    one_group(sx)
    for copy in copies:
        copy.wait()

    def add_up(place):
        total = parts[sx, place].astype(jnp.float32)
        for step in range(xcount - 1):
            total = total + x_in[step, place].astype(jnp.float32)
        return total

    copies = []
    for step in range(1, zcount):
        to = (sz + step) % zcount
        mid[step - 1] = add_up(to).astype(jnp.bfloat16)
        copies.append(
            exchange(mid.at[step - 1], z_in.at[step - 1], s7.at[step - 1], r7.at[step - 1], at_xz(to, sx))
        )
        copies[-1].start()
    total = add_up(sz)
    for copy in copies:
        copy.wait()
    for step in range(zcount - 1):
        total = total + z_in[step].astype(jnp.float32)
    out[...] = total


def process(tiles, flags, src_chan, ycount, xcount, zcount, out_scale):
    seg_count, chan_count = flags.shape
    per = chan_count // (xcount * zcount)
    dtype = tiles.dtype
    slab = (NSRC * seg_count // (2 * ycount), SLOW, FAST)
    half = (ycount,) + slab
    result = (per, NSRC, SLOW, FAST)
    dma = pltpu.SemaphoreType.DMA
    vmem = pltpu.VMEM
    spec = pl.BlockSpec(memory_space=pltpu.VMEM)
    smem = pl.BlockSpec(memory_space=pltpu.SMEM)
    operands = (
        (tiles, flags, jnp.asarray(np.eye(chan_count), jnp.float32)) + tables(out_scale)
    )
    return pl.pallas_call(
        functools.partial(whole_kernel, ycount, xcount, zcount),
        out_shape=jax.ShapeDtypeStruct(result, jnp.float32),
        in_specs=[smem, smem] + [spec] * len(operands),
        out_specs=spec,
        scratch_shapes=[
            vmem((2, seg_count, chan_count, SLOW, FAST), jnp.float32),
            vmem((3, seg_count, NSRC, SLOW, FAST), jnp.float32),
            vmem((seg_count * chan_count // 8, 8, FAST), jnp.float32),
            vmem((2,) + half, dtype),
            vmem(half, dtype),
            vmem(half, dtype),
            vmem((ycount - 1,) + slab, dtype),
            vmem(slab, dtype),
            vmem(slab, dtype),
            vmem(half, dtype),
            vmem(half, dtype),
            vmem((xcount, zcount) + result, dtype),
            vmem((xcount - 1, zcount) + result, dtype),
            vmem((zcount - 1,) + result, dtype),
            vmem((zcount - 1,) + result, dtype),
            dma,
            dma,
            dma((ycount - 1,)),
            dma((ycount - 1,)),
            dma,
            dma,
            dma((ycount - 1,)),
            dma((ycount - 1,)),
            dma,
            dma,
            dma((xcount - 1,)),
            dma((xcount - 1,)),
            dma((zcount - 1,)),
            dma((zcount - 1,)),
        ],
        compiler_params=pltpu.CompilerParams(
            collective_id=0, has_side_effects=True, vmem_limit_bytes=VMEM_LIMIT
        ),
        name="process",
    )(src_chan, flags, *operands)


def per_device(recordings, valid_mask, src_chan):
    chan_count, seg_count, samples = recordings.shape
    group_count = lax.axis_size("tm")
    xcount = 4
    zcount = group_count // xcount
    ycount = lax.axis_size("chan") // 4
    out_scale = 1.0 / math.sqrt(samples * seg_count * group_count)
    tiles = jnp.transpose(recordings, (1, 0, 2))
    tiles = tiles.reshape(seg_count, chan_count // 8, 8, SLOW, FAST)
    tiles = jnp.transpose(tiles, (0, 1, 3, 2, 4))
    tiles = tiles.reshape(seg_count * chan_count // 8, 8 * SLOW, FAST)
    flags = jnp.transpose(valid_mask)
    summed = process(tiles, flags, src_chan, ycount, xcount, zcount, out_scale)
    return jnp.transpose(summed, (1, 0, 2, 3)).reshape(NSRC, chan_count // group_count, samples)


def solution(mesh):
    return jax.shard_map(
        per_device,
        mesh=mesh,
        in_specs=(P("chan", "tm", None), P("chan", "tm"), P()),
        out_specs=P(None, ("chan", "tm"), None),
        check_vma=False,
    )
```

time: 81 us -> 70.4 us (0.87)
  Pallas kernels: 73.9 us -> 68.6 us
  local copies, waits for them, and re-layouts: 6.11 us -> 1.71 us
    unnamed x1 -> x0, local copies, waits for them, and re-layouts: 4.4 us -> none
    pallas_call x1 -> x0, Pallas kernels: 3.95 us -> none  [pick(): pl.pallas_call(pick_kernel, grid_spec=pltpu.PrefetchScalarGridSpec(num_sc...]
    pallas_call x1, Pallas kernels: 70 us -> 68.6 us  [process(): pl.pallas_call(functools.partial(whole_kernel, ycount, xcount, zcount), o...]
where the time goes in v4:
time: 70.4 us; the launch traced here: 70.3 us
  Pallas kernels  68.6 us (97%)
  local copies, waits for them, and re-layouts  1.71 us (2%)
    pallas_call x1, Pallas kernels, process(): pl.pallas_call(functools.partial(whole_kernel, ycount, xcount, zcount), o...  68.6 us
    reshape x2, local copies, waits for them, and re-layouts, per_device(): jnp.transpose(summed, (1, 0, 2, 3))  1.71 us

profile of v4, /device:TPU:2, one launch (start us, length us, event | category | flops | bytes accessed | tf_op | source)
XLA Modules:
  0.0 70.3 jit_solution(14595042553474434551)
XLA Ops:
  0.0 68.6 %process.1 = f32[2,4,32,128]{3,2,1,0:T(8,128)} custom-call(s32[4]{0:T(128)} %src.1, s32[12,32]{1,0:T(8,128)} %bitcast.15, bf16[48,256,128]{2,1,0:T(8,128)(2,1)} %bitcast.13, s32[12,32]{1,0:T(8,128)} %bitcast.16, f32[32,32]{1,0:T(8,128)} %constant.16.clone.eye, bf16[512,256]{1,0:T(8,128)(2,1)} %constant.17.clone.first, ...), custom_call_target="tpu_custom_call" | custom-call | tf_op jit(solution)/shard_map/process/pallas_call | solution.py:351
  68.6 0.9 %reshape.11 = f32[4,2,4096]{2,0,1:T(4,128)S(1)} reshape(f32[4,2,32,128]{3,2,0,1:T(8,128)} %bitcast.14) | data formatting | bytes 262144 | tf_op jit(solution)/shard_map/reshape | solution.py:407
  69.6 0.8 %copy.12 = f32[4,2,4096]{2,1,0:T(2,128)} copy(f32[4,2,4096]{2,0,1:T(4,128)S(1)} %reshape.11) | data formatting | bytes 262144 | tf_op jit(solution)/shard_map/reshape | solution.py:407

commit v5 on v4

--- a/solution.py
+++ b/solution.py
@@ -13,6 +13,7 @@
 SLOW = 32
 FAST = 128
 BLOCK = 6
+UNROLL = 6
 MESH = pl.DeviceIdType.MESH
 VMEM_LIMIT = 60 * 1024 * 1024
 
@@ -101,7 +102,7 @@
     ycount, xcount, zcount,
     src, marks, tiles, flags, eye, first, first_by_n, second, back, outer, twist, turn,
     out,
-    white, source, weights, own,
+    white, source, weights, own, cross,
     pair_in, half, slices_in, part, across_in, whole, twin,
     parts, x_in, mid, z_in,
     s1, r1, s2, r2, s3, r3, s4, r4, s5, r5, s6, r6, s7, r7,
@@ -239,36 +240,32 @@
 
     per = parts.shape[2]
 
-    def some_channels(chan, to, place):
-        real_rows = [[] for _ in range(per)]
-        imag_rows = [[] for _ in range(per)]
-        for strip in range(SLOW // 8):
-            rows = slice(strip * 8, strip * 8 + 8)
-            sums = [[None] * 3 for _ in range(per)]
-            for seg in range(seg_count):
+    def some_channels(chan, place):
+        def one_strip(strip, carry):
+            rows = pl.ds(pl.multiple_of(strip * 8, 8), 8)
+
+            def one_segment(seg, sums):
                 terms = [source[k, seg, :, rows] for k in range(3)]
+                new = []
                 for which in range(per):
                     w_real = white[0, seg, chan + which, rows]
                     w_imag = white[1, seg, chan + which, rows]
                     for k, factor in enumerate((w_real + w_imag, w_imag, w_real)):
-                        now = terms[k] * factor[None]
-                        sums[which][k] = now if seg == 0 else sums[which][k] + now
+                        new.append(sums[3 * which + k] + terms[k] * factor[None])
+                return tuple(new)
+
+            zero = jnp.zeros((NSRC, 8, FAST), jnp.float32)
+            sums = lax.fori_loop(0, seg_count, one_segment, (zero,) * (3 * per), unroll=UNROLL)
             for which in range(per):
-                real_rows[which].append(sums[which][0] - sums[which][1])
-                imag_rows[which].append(sums[which][0] - sums[which][2])
-        both = jnp.concatenate(
-            [
-                jnp.concatenate(
-                    [
-                        jnp.concatenate(real_rows[which], axis=1).astype(jnp.bfloat16),
-                        jnp.concatenate(imag_rows[which], axis=1).astype(jnp.bfloat16),
-                    ],
-                    axis=2,
-                ).reshape(NSRC * SLOW, 2 * FAST)
-                for which in range(per)
-            ],
-            axis=0,
-        )
+                base, less, more = sums[3 * which : 3 * which + 3]
+                cross[place, which, :, rows, :FAST] = base - less
+                cross[place, which, :, rows, FAST:] = base - more
+            return carry
+
+        lax.fori_loop(0, SLOW // 8, one_strip, 0)
+
+    def finish(to, place):
+        both = cross[place].astype(jnp.bfloat16).reshape(per * NSRC * SLOW, 2 * FAST)
         v = jnp.dot(both, back[...], preferred_element_type=jnp.float32)
         v_real = v[:, :FAST].reshape(per * NSRC, SLOW, FAST)
         v_imag = v[:, FAST:].reshape(per * NSRC, SLOW, FAST)
@@ -295,10 +292,12 @@
 
     def one_group(to):
         def one(place, carry):
-            some_channels(per * (place * xcount + to), to, place)
+            some_channels(per * (place * xcount + to), place)
             return carry
 
         lax.fori_loop(0, zcount, one, 0)
+        for place in range(zcount):
+            finish(to, place)
 
     copies = []
     for step in range(1, xcount):
@@ -358,6 +357,7 @@
             vmem((3, seg_count, NSRC, SLOW, FAST), jnp.float32),
             vmem((seg_count * chan_count // 8, 8, FAST), jnp.float32),
             vmem((2,) + half, dtype),
+            vmem((zcount, per, NSRC, SLOW, 2 * FAST), jnp.float32),
             vmem(half, dtype),
             vmem(half, dtype),
             vmem((ycount - 1,) + slab, dtype),

time: 70.4 us -> 69.5 us (0.987)
  Pallas kernels: 68.6 us -> 67.7 us
    pallas_call x1, Pallas kernels: 68.6 us -> 67.7 us  [process(): pl.pallas_call(functools.partial(whole_kernel, ycount, xcount, zcount), o...]
where the time goes in v5:
time: 69.5 us; the launch traced here: 69.4 us
  Pallas kernels  67.7 us (97%)
  local copies, waits for them, and re-layouts  1.71 us (2%)
    pallas_call x1, Pallas kernels, process(): pl.pallas_call(functools.partial(whole_kernel, ycount, xcount, zcount), o...  67.7 us
    reshape x2, local copies, waits for them, and re-layouts, per_device(): jnp.transpose(summed, (1, 0, 2, 3))  1.71 us

profile of v5, /device:TPU:2, one launch (start us, length us, event | category | flops | bytes accessed | tf_op | source)
XLA Modules:
  0.0 69.4 jit_solution(18158715203263246285)
XLA Ops:
  0.0 67.7 %process.1 = f32[2,4,32,128]{3,2,1,0:T(8,128)} custom-call(s32[4]{0:T(128)} %src.1, s32[12,32]{1,0:T(8,128)} %bitcast.15, bf16[48,256,128]{2,1,0:T(8,128)(2,1)} %bitcast.13, s32[12,32]{1,0:T(8,128)} %bitcast.16, f32[32,32]{1,0:T(8,128)} %constant.16.clone.eye, bf16[512,256]{1,0:T(8,128)(2,1)} %constant.17.clone.first, ...), custom_call_target="tpu_custom_call" | custom-call | tf_op jit(solution)/shard_map/process/pallas_call | solution.py:350
  67.7 0.9 %reshape.11 = f32[4,2,4096]{2,0,1:T(4,128)S(1)} reshape(f32[4,2,32,128]{3,2,0,1:T(8,128)} %bitcast.14) | data formatting | bytes 262144 | tf_op jit(solution)/shard_map/reshape | solution.py:407
  68.6 0.8 %copy.12 = f32[4,2,4096]{2,1,0:T(2,128)} copy(f32[4,2,4096]{2,0,1:T(4,128)S(1)} %reshape.11) | data formatting | bytes 262144 | tf_op jit(solution)/shard_map/reshape | solution.py:407

commit v6 on v5

--- a/solution.py
+++ b/solution.py
@@ -216,14 +216,21 @@
             )
         )
         copies[-1].start()
+    mirrors = [exchange(whole.at[y], twin.at[y], s5.at[0], r5.at[0], sibling)]
+    mirrors[0].start()
     forward(5, 7)
+    for step in range(1, ycount):
+        copies[step - 1].wait_recv()
+        came = (y + ycount - step) % ycount
+        mirrors.append(
+            exchange(whole.at[came], twin.at[came], s5.at[step], r5.at[step], sibling)
+        )
+        mirrors[-1].start()
+    forward(7, seg_count * sets // BLOCK)
     for copy in copies:
+        copy.wait_send()
+    for copy in mirrors:
         copy.wait()
-
-    copy = exchange(whole, twin, s5, r5, sibling)
-    copy.start()
-    forward(7, seg_count * sets // BLOCK)
-    copy.wait()
 
     low = jnp.where(core == 0, whole[...], twin[...])
     high = jnp.where(core == 0, twin[...], whole[...])
@@ -377,8 +384,8 @@
             dma,
             dma((ycount - 1,)),
             dma((ycount - 1,)),
-            dma,
-            dma,
+            dma((ycount,)),
+            dma((ycount,)),
             dma((xcount - 1,)),
             dma((xcount - 1,)),
             dma((zcount - 1,)),

time: 69.5 us -> 69.5 us (level)
  no operation moved by 1% of the time
where the time goes in v6:
time: 69.5 us; the launch traced here: 69.4 us
  Pallas kernels  67.6 us (97%)
  local copies, waits for them, and re-layouts  1.71 us (2%)
    pallas_call x1, Pallas kernels, process(): pl.pallas_call(functools.partial(whole_kernel, ycount, xcount, zcount), o...  67.6 us
    reshape x2, local copies, waits for them, and re-layouts, per_device(): jnp.transpose(summed, (1, 0, 2, 3))  1.71 us

profile of v6, /device:TPU:2, one launch (start us, length us, event | category | flops | bytes accessed | tf_op | source)
XLA Modules:
  0.0 69.4 jit_solution(16789826984427610627)
XLA Ops:
  0.0 67.6 %process.1 = f32[2,4,32,128]{3,2,1,0:T(8,128)} custom-call(s32[4]{0:T(128)} %src.1, s32[12,32]{1,0:T(8,128)} %bitcast.15, bf16[48,256,128]{2,1,0:T(8,128)(2,1)} %bitcast.13, s32[12,32]{1,0:T(8,128)} %bitcast.16, f32[32,32]{1,0:T(8,128)} %constant.16.clone.eye, bf16[512,256]{1,0:T(8,128)(2,1)} %constant.17.clone.first, ...), custom_call_target="tpu_custom_call" | custom-call | tf_op jit(solution)/shard_map/process/pallas_call | solution.py:357
  67.6 0.9 %reshape.11 = f32[4,2,4096]{2,0,1:T(4,128)S(1)} reshape(f32[4,2,32,128]{3,2,0,1:T(8,128)} %bitcast.14) | data formatting | bytes 262144 | tf_op jit(solution)/shard_map/reshape | solution.py:414
  68.6 0.8 %copy.12 = f32[4,2,4096]{2,1,0:T(2,128)} copy(f32[4,2,4096]{2,0,1:T(4,128)S(1)} %reshape.11) | data formatting | bytes 262144 | tf_op jit(solution)/shard_map/reshape | solution.py:414
